TPU v7x, 256 devices: a whole 4x4x8 slice. The times are simulated.
256 devices in a mesh: hel: 4 (over z_lo), rad: 64 (over z_hi, y, x, core).
Axes of the slice: x: 4, y: 4, z: 8 (z_hi: 2, z_lo: 4; z = z_hi * 4 + z_lo), core: 2. Of those that a mesh axis runs over, the one named last changes fastest.
Arguments:
- packet: float32 [2, 8, 1024, 8, 1024], P(None, 'hel', 'rad'), may hold values from -6 to 6
- radial_weight: float32 [8, 1024], P(None, 'rad'), may hold values from 0.25 to 1.75
- tile_blocks: float32 [24, 128, 128], replicated, may hold values from -0.1875 to 0.1875
- tile_list: int32 [24, 3], replicated, may hold values from 0 to 7, as said below
- coupling: float32 [8, 1024], replicated, may hold values from 0.1 to 0.5
Outputs:
- advanced: float32 [2, 8, 1024, 8, 1024], P(None, 'hel', 'rad')
Inputs may be any that keep to these rules, and one draw needn't show every extreme that they name: `tile_list`: each row is (block row, block column, radial weight index): block indices lie below 8 and weight indices below 8; every block row and every weight index occurs in some row; rows may repeat pairs.
All inputs are finite; a program needn't handle non-finite values.
Results may differ from a plain program's by a relative error of at most 0.0001.
Values sent between devices are 32-bit elements; how exact they have to be, the bound alone decides.
A program may use at most 128 MiB of HBM per device.

v0:
```python
import jax
import jax.numpy as jnp
from jax import lax
from jax.sharding import PartitionSpec as P

R = 1024
TILE = 128
TAYLOR = 3


kinetic_scale = 0.5


def extended(block, sides, width):
    for axis, dim in sides:
        count = lax.axis_size(axis)
        forward = [(i, i + 1) for i in range(count - 1)]
        backward = [(target, source) for source, target in forward]
        low = lax.ppermute(
            lax.slice_in_dim(block, block.shape[dim] - width, None, axis=dim), axis, forward
        )
        high = lax.ppermute(lax.slice_in_dim(block, 0, width, axis=dim), axis, backward)
        block = jnp.concatenate([low, block, high], axis=dim)
    return block


def potential(term, radial_weight, tile_blocks, tile_list):
    term_shape = term.shape
    blocks = term.reshape(
        term_shape[0], term_shape[1], term_shape[2], term_shape[3], term_shape[4] // TILE, TILE
    )

    def add_tile(position, summed):
        target = tile_list[position, 0]
        source = tile_list[position, 1]
        weight_row = tile_list[position, 2]
        source_block = lax.dynamic_index_in_dim(blocks, source, 4, keepdims=False)
        matrix = lax.dynamic_index_in_dim(tile_blocks, position, 0, keepdims=False)
        product = jnp.einsum(
            "ckrvi,ij->ckrvj", source_block, matrix, precision=lax.Precision.HIGHEST
        )
        factor = lax.dynamic_index_in_dim(radial_weight, weight_row, 0, keepdims=False)
        product = product * factor[None, None, :, None, None]
        current = lax.dynamic_index_in_dim(summed, target, 4, keepdims=False)
        return lax.dynamic_update_index_in_dim(summed, current + product, target, 4)

    summed = lax.fori_loop(0, tile_list.shape[0], add_tile, jnp.zeros(blocks.shape, jnp.float32))
    return summed.reshape(term_shape)


def coriolis_rim(term, coupling, radial_factor):
    helices = term.shape[1]
    padded = extended(term, (("hel", 1),), 1)
    first_helix = lax.axis_index("hel") * helices
    coupled = jnp.concatenate([jnp.zeros((1, coupling.shape[1]), jnp.float32), coupling], axis=0)
    window = lax.dynamic_slice_in_dim(coupled, first_helix, helices + 1, 0)
    lower = window[:helices]
    upper = window[1:]
    mixed = (
        upper[None, :, None, None, :] * padded[:, 2:]
        + lower[None, :, None, None, :] * padded[:, :-2]
    )
    return mixed * radial_factor[None, None, :, None, None]


def transform(matrix, moving):
    return jnp.einsum("qr,cnrm->cnqm", matrix, moving, precision=lax.Precision.HIGHEST)


def propagate(moving, cosine_table, sine_table, phase_cos, phase_sin):
    length = moving.shape[2]
    cos_part = transform(cosine_table, moving)
    sin_part = transform(sine_table, moving)
    spec_real = cos_part[0] + sin_part[1]
    spec_imag = cos_part[1] - sin_part[0]
    turn_cos = phase_cos[None, :, None]
    turn_sin = phase_sin[None, :, None]
    turned = jnp.stack(
        [turn_cos * spec_real + turn_sin * spec_imag, turn_cos * spec_imag - turn_sin * spec_real]
    )
    cos_back = transform(cosine_table, turned)
    sin_back = transform(sine_table, turned)
    return jnp.stack([(cos_back[0] - sin_back[1]) / length, (cos_back[1] + sin_back[0]) / length])


def expand(current, radial_weight, tile_blocks, tile_list, coupling, radial_factor, coriolis):
    advanced = current
    for degree in range(1, TAYLOR + 1):
        applied = potential(current, radial_weight, tile_blocks, tile_list) + coriolis(
            current, coupling, radial_factor
        )
        current = jnp.stack([applied[1], -applied[0]]) / degree
        advanced = advanced + current
    return advanced


def body(packet, radial_weight, tile_blocks, tile_list, coupling):
    two_parts, helices, radial, vibration, channels = packet.shape
    wave_index = jnp.arange(R, dtype=jnp.int32)
    angle_table = (wave_index[:, None] * wave_index[None, :] % R).astype(jnp.float32) * (
        2.0 * jnp.pi / R
    )
    cosine_table = jnp.cos(angle_table)
    sine_table = jnp.sin(angle_table)
    signed = jnp.where(wave_index < R // 2, wave_index, wave_index - R).astype(jnp.float32)
    phase_angle = kinetic_scale * (2.0 * jnp.pi * signed / R) ** 2
    phase_cos = jnp.cos(phase_angle)
    phase_sin = jnp.sin(phase_angle)
    flattened = packet.reshape(two_parts, helices, radial, vibration * channels)
    moved = propagate(
        lax.all_to_all(flattened, "rad", split_axis=3, concat_axis=2, tiled=True),
        cosine_table,
        sine_table,
        phase_cos,
        phase_sin,
    )
    returned = lax.all_to_all(moved, "rad", split_axis=2, concat_axis=3, tiled=True)
    current = returned.reshape(packet.shape)
    distance = (lax.axis_index("rad") * radial + jnp.arange(radial, dtype=jnp.int32)).astype(
        jnp.float32
    )
    radial_factor = 1.0 / (1.0 + 3.0 * distance / R) ** 2
    return expand(
        current, radial_weight, tile_blocks, tile_list, coupling, radial_factor, coriolis_rim
    )


def solution(mesh):
    in_specs = (P(None, "hel", "rad", None, None), P(None, "rad"), P(), P(), P())
    out_specs = P(None, "hel", "rad", None, None)
    return jax.shard_map(body, mesh=mesh, in_specs=in_specs, out_specs=out_specs, check_vma=False)
```

profile of v0, /device:TPU:1, one launch (start us, length us, event | category | flops | bytes accessed | tf_op | source)
XLA Modules:
  0.0 1131.0 jit_solution(3895176065633893081)
XLA Ops:
  0.0 13.9 %copy.43 = f32[2,2,16,8,1024]{2,1,0,4,3:T(2,128)} copy(f32[2,2,16,8,1024]{4,3,2,1,0:T(8,128)} %param.11) | data formatting | bytes 4194304 | tf_op args[0]
  13.9 25.5 %reshape.66 = f32[64,1,8192]{2,1,0:T(1,128)} reshape(f32[8192,2,2,16]{3,2,1,0:T(2,128)} %bitcast.187) | data formatting | bytes 4194304
  39.5 15.6 %all-to-all-start = ((f32[64,1,8192]{2,1,0:T(1,128)}), f32[64,1,8192]{2,1,0:T(1,128)S(1)}, u32[]{:S(2)}, u32[]{:S(2)}) async-start(f32[64,1,8192]{2,1,0:T(1,128)} %reshape.66), calls=%async_computation | async-start | bytes 4194304 | tf_op jit(solution)/shard_map/all_to_all | solution.py:111
  55.1 37.8 %all-to-all-done = f32[64,1,8192]{2,1,0:T(1,128)S(1)} async-done(((f32[64,1,8192]{2,1,0:T(1,128)}), f32[64,1,8192]{2,1,0:T(1,128)S(1)}, u32[]{:S(2)}, u32[]{:S(2)}) %all-to-all-start) | async-done | bytes 2097184 | tf_op jit(solution)/shard_map/all_to_all | solution.py:111
  94.8 7.5 reduce
  102.3 23.7 %reshape.67 = f32[8192,2,2,16]{3,2,1,0:T(2,128)} reshape(f32[64,8192]{1,0:T(8,128)S(1)} %reduce) | data formatting | bytes 4194304
  126.0 17.9 %copy.68 = f32[2,2,16,64,128]{4,2,3,1,0:T(8,128)S(1)} copy(f32[2,2,16,64,128]{2,1,0,4,3:T(2,128)} %bitcast.186) | data formatting | bytes 4194304 | tf_op jit(solution)/shard_map/all_to_all | solution.py:111
  143.9 22.5 %fusion.63 = f32[2,2,1024,128]{3,2,1,0:T(8,128)S(1)} fusion(f32[2,2,1024,128]{3,2,1,0:T(8,128)S(1)} %bitcast.190), kind=kOutput, calls=%fused_computation.102 | convolution fusion | flops 6457131008 | bytes 4194304 | tf_op jit(solution)/shard_map/qr,cnrm->cnqm/dot_general | solution.py:67
  166.4 22.1 %fusion.69 = f32[2,2,1024,128]{3,2,1,0:T(8,128)S(1)} fusion(f32[2,2,1024,128]{3,2,1,0:T(8,128)S(1)} %bitcast.191), kind=kOutput, calls=%fused_computation.104 | convolution fusion | flops 6457131008 | bytes 4194304 | tf_op jit(solution)/shard_map/qr,cnrm->cnqm/dot_general | solution.py:67
  188.9 29.1 %fusion.72 = f32[2,2,1024,128]{2,3,1,0:T(8,128)S(1)} fusion(f32[1,2,1024,128]{3,2,1,0:T(8,128)S(1)} %get-tuple-element.399, f32[1,2,1024,128]{3,2,1,0:T(8,128)S(1)} %get-tuple-element.398), kind=kOutput, calls=%fused_computation.105 | convolution fusion | flops 6457655296 | bytes 4194304 | tf_op jit(solution)/shard_map/qr,cnrm->cnqm/dot_general | solution.py:67
  218.1 29.3 %fusion.66 = f32[2,2,1024,128]{2,3,1,0:T(8,128)S(1)} fusion(f32[1,2,1024,128]{3,2,1,0:T(8,128)S(1)} %get-tuple-element.399, f32[1,2,1024,128]{3,2,1,0:T(8,128)S(1)} %get-tuple-element.398), kind=kOutput, calls=%fused_computation.103 | convolution fusion | flops 6457655296 | bytes 4194304 | tf_op jit(solution)/shard_map/qr,cnrm->cnqm/dot_general | solution.py:67
  248.0 2.3 copy.48
  250.3 16.9 %all-to-all-start.1 = ((f32[2,2,1024,128]{3,1,0,2:T(2,128)}), f32[2,2,1024,128]{3,1,0,2:T(2,128)}, u32[]{:S(2)}, u32[]{:S(2)}) async-start(f32[2,2,1024,128]{3,1,0,2:T(2,128)} %copy.48), calls=%async_computation.1 | async-start | bytes 4194304 | tf_op jit(solution)/shard_map/all_to_all | solution.py:117
  267.3 31.5 %all-to-all-done.1 = f32[2,2,1024,128]{3,1,0,2:T(2,128)} async-done(((f32[2,2,1024,128]{3,1,0,2:T(2,128)}), f32[2,2,1024,128]{3,1,0,2:T(2,128)}, u32[]{:S(2)}, u32[]{:S(2)}) %all-to-all-start.1) | async-done | bytes 2097184 | tf_op jit(solution)/shard_map/all_to_all | solution.py:117
  308.6 31.4 %collective-permute-start.1 = (f32[2,1,16,8,1024]{4,3,2,1,0:T(8,128)}, f32[2,1,16,8,1024]{4,3,2,1,0:T(8,128)}, u32[]{:S(2)}, u32[]{:S(2)}) collective-permute-start(f32[2,1,16,8,1024]{4,3,2,1,0:T(8,128)} %get-tuple-element.417), channel_id=1, source_target_pairs={{0,64},{64,128},{128,192},{1,65},{65,129},{129,193},{2,66},{66,130... | collective-permute-start | bytes 3145736 | tf_op jit(solution)/shard_map/ppermute | solution.py:19
  341.5 258.9 %while.39 = (s32[]{:T(128)}, f32[2,2,16,8,8,128]{5,3,4,2,1,0:T(8,128)}, s32[24,3]{0,1:T(4,128)S(1)}, f32[2,2,16,8,8,128]{5,2,4,3,1,0:T(8,128)}, f32[24,128,128]{...) while((s32[]{:T(128)}, f32[2,2,16,8,8,128]{5,3,4,2,1,0:T(8,128)}, ...), condition=%wide.region_1.2_spmd, body=%wide.region_0.1_spmd.sunk | while | flops 100794376 | bytes 1901487 | solution.py:47
  600.5 3.0 fusion.55
  606.9 5.0 collective-permute-start.3
  614.9 249.4 %while.40 = (s32[]{:T(128)}, f32[2,2,16,8,8,128]{5,3,4,2,1,0:T(8,128)}, s32[24,3]{0,1:T(4,128)S(1)}, f32[2,2,16,8,8,128]{5,3,4,2,1,0:T(8,128)}, f32[24,128,128]{...) while((s32[]{:T(128)}, f32[2,2,16,8,8,128]{5,3,4,2,1,0:T(8,128)}, ...), condition=%wide.region_3.4_spmd, body=%wide.region_2.3_spmd.sunk | while | flops 100794376 | bytes 1377199 | solution.py:47
  864.4 3.3 fusion.50
  872.8 5.0 collective-permute-start.5
  881.0 241.7 %while.41 = (s32[]{:T(128)}, f32[2,2,16,8,8,128]{5,3,4,2,1,0:T(8,128)}, s32[24,3]{0,1:T(4,128)S(1)}, f32[2,2,16,8,8,128]{5,3,2,1,0,4:T(8,128)}, f32[24,128,128]{...) while((s32[]{:T(128)}, f32[2,2,16,8,8,128]{5,3,4,2,1,0:T(8,128)}, ...), condition=%wide.region_5.6_spmd, body=%wide.region_4.5_spmd.sunk | while | flops 100794376 | bytes 1377199 | solution.py:47
  1122.7 3.6 fusion.45
  1128.3 2.3 fusion.41
  (365 shorter events, 366.5 us)
Async XLA Ops:
  39.5 53.4 %all-to-all-start = ((f32[64,1,8192]{2,1,0:T(1,128)}), f32[64,1,8192]{2,1,0:T(1,128)S(1)}, u32[]{:S(2)}, u32[]{:S(2)}) async-start(f32[64,1,8192]{2,1,0:T(1,128)} %reshape.66), calls=%async_computation | async-start | bytes 4194304 | tf_op jit(solution)/shard_map/all_to_all | solution.py:111
  92.9 1.3 copy-start.8
  250.3 16.9 %copy-start.10 = (f32[8,1024]{1,0:T(8,128)S(1)}, f32[8,1024]{1,0:T(8,128)}, u32[]{:S(2)}) copy-start(f32[8,1024]{1,0:T(8,128)} %param.15) | copy-start | bytes 98308
  250.3 48.5 %all-to-all-start.1 = ((f32[2,2,1024,128]{3,1,0,2:T(2,128)}), f32[2,2,1024,128]{3,1,0,2:T(2,128)}, u32[]{:S(2)}, u32[]{:S(2)}) async-start(f32[2,2,1024,128]{3,1,0,2:T(2,128)} %copy.48), calls=%async_computation.1 | async-start | bytes 4194304 | tf_op jit(solution)/shard_map/all_to_all | solution.py:117
  300.5 1.4 copy-start.3
  307.1 34.4 %copy-start.9 = (s32[24,3]{0,1:T(4,128)S(1)}, s32[24,3]{0,1:T(4,128)}, u32[]{:S(2)}) copy-start(s32[24,3]{0,1:T(4,128)} %param.14) | copy-start | bytes 868
  307.1 293.3 %collective-permute-start = (f32[2,1,16,8,1024]{4,3,2,1,0:T(8,128)}, f32[2,1,16,8,1024]{4,3,2,1,0:T(8,128)}, u32[]{:S(2)}, u32[]{:S(2)}) collective-permute-start(f32[2,1,16,8,1024]{4,3,2,1,0:T(8,128)} %get-tuple-element.416), channel_id=1, source_target_pairs={{64,0},{128,64},{192,128},{65,1},{129,65},{193,129},{66,2},{130,66... | collective-permute-start | bytes 3145736 | tf_op jit(solution)/shard_map/ppermute | solution.py:22
  308.6 291.9 %collective-permute-start.1 = (f32[2,1,16,8,1024]{4,3,2,1,0:T(8,128)}, f32[2,1,16,8,1024]{4,3,2,1,0:T(8,128)}, u32[]{:S(2)}, u32[]{:S(2)}) collective-permute-start(f32[2,1,16,8,1024]{4,3,2,1,0:T(8,128)} %get-tuple-element.417), channel_id=1, source_target_pairs={{0,64},{64,128},{128,192},{1,65},{65,129},{129,193},{2,66},{66,130... | collective-permute-start | bytes 3145736 | tf_op jit(solution)/shard_map/ppermute | solution.py:19
  603.9 1.7 copy-start.1
  605.6 258.7 %collective-permute-start.2 = (f32[2,1,16,8,1024]{4,3,2,1,0:T(8,128)}, f32[2,1,16,8,1024]{4,3,2,1,0:T(8,128)}, u32[]{:S(2)}, u32[]{:S(2)}) collective-permute-start(f32[2,1,16,8,1024]{4,3,2,1,0:T(8,128)} %get-tuple-element.414), channel_id=1, source_target_pairs={{64,0},{128,64},{192,128},{65,1},{129,65},{193,129},{66,2},{130,66... | collective-permute-start | bytes 3145736 | tf_op jit(solution)/shard_map/ppermute | solution.py:22
  606.9 257.5 %collective-permute-start.3 = (f32[2,1,16,8,1024]{4,3,2,1,0:T(8,128)}, f32[2,1,16,8,1024]{4,3,2,1,0:T(8,128)}, u32[]{:S(2)}, u32[]{:S(2)}) collective-permute-start(f32[2,1,16,8,1024]{4,3,2,1,0:T(8,128)} %get-tuple-element.415), channel_id=1, source_target_pairs={{0,64},{64,128},{128,192},{1,65},{65,129},{129,193},{2,66},{66,130... | collective-permute-start | bytes 3145736 | tf_op jit(solution)/shard_map/ppermute | solution.py:19
  868.2 1.0 copy-start.4
  868.2 1.3 copy-start.6
  869.5 2.0 copy-start
  871.5 251.2 %collective-permute-start.4 = (f32[2,1,16,8,1024]{4,3,2,1,0:T(8,128)}, f32[2,1,16,8,1024]{4,3,2,1,0:T(8,128)}, u32[]{:S(2)}, u32[]{:S(2)}) collective-permute-start(f32[2,1,16,8,1024]{4,3,2,1,0:T(8,128)} %get-tuple-element.408), channel_id=1, source_target_pairs={{64,0},{128,64},{192,128},{65,1},{129,65},{193,129},{66,2},{130,66... | collective-permute-start | bytes 3145736 | tf_op jit(solution)/shard_map/ppermute | solution.py:22
  872.8 249.9 %collective-permute-start.5 = (f32[2,1,16,8,1024]{4,3,2,1,0:T(8,128)}, f32[2,1,16,8,1024]{4,3,2,1,0:T(8,128)}, u32[]{:S(2)}, u32[]{:S(2)}) collective-permute-start(f32[2,1,16,8,1024]{4,3,2,1,0:T(8,128)} %get-tuple-element.409), channel_id=1, source_target_pairs={{0,64},{64,128},{128,192},{1,65},{65,129},{129,193},{2,66},{66,130... | collective-permute-start | bytes 3145736 | tf_op jit(solution)/shard_map/ppermute | solution.py:19
  1126.4 1.2 copy-start.2
  1126.4 1.5 copy-start.5
  1126.4 1.8 copy-start.7
where the time goes:
time: 1150 us; the launch traced here: 1130 us
  loops' own time  414 us (36%)
  local copies, waits for them, and re-layouts  294 us (26%)
  matrix products  247 us (21%)
  starting transfers between devices  77.9 us (7%)
  waiting for transfers between devices  69.3 us (6%)
  other arithmetic  27 us (2%)
    another operation x3, loops' own time, potential(): lax.fori_loop(0, tile_list.shape[0], add_tile, jnp.zeros(blocks.shape, jn...  414 us
    dot_general x72, matrix products, add_tile(): jnp.einsum('ckrvi,ij->ckrvj', source_block, matrix, precision=lax.Precisi...  144 us
    dot_general x4, matrix products, transform(): jnp.einsum('qr,cnrm->cnqm', matrix, moving, precision=lax.Precision.HIGHEST)  103 us
    dynamic_slice x72, local copies, waits for them, and re-layouts, add_tile(): current = lax.dynamic_index_in_dim(summed, target, 4, keepdims=False)  70.1 us
    unnamed x25, local copies, waits for them, and re-layouts  68.9 us
    mul x72, local copies, waits for them, and re-layouts, add_tile(): product = product * factor[None, None, :, None, None]  50.1 us
    dynamic_slice x72, local copies, waits for them, and re-layouts, add_tile(): weight_row = tile_list[position, 2]  47.6 us
    ppermute x3, starting transfers between devices, extended(): lax.ppermute(lax.slice_in_dim(block, block.shape[dim] - width, None, axis...  41.4 us
  transfers between devices with their start and end apart: 8, of which 2 were waited for; matrix products, arithmetic and copies ran while one was open for 30% of the time, Pallas kernels for 0%

commit v1 on v0

v1 whole, which is shorter than its diff:
```python
import functools

import jax
import jax.numpy as jnp
import ml_dtypes
import numpy as np
from jax import lax
from jax.experimental import pallas as pl
from jax.experimental.pallas import tpu as pltpu
from jax.sharding import PartitionSpec as P

R = 1024
HALF = R // 2
TILE = 128
TAYLOR = 3
NT = 24
K = 8
V = 8
CB = 8
Q = 8
MESH = pl.DeviceIdType.MESH
F32 = jnp.float32
BF16 = jnp.bfloat16

kinetic_scale = 0.5


def propagator_tables():
    wave = np.arange(R)
    signed = np.where(wave < R // 2, wave, wave - R).astype(np.float64)
    angle = kinetic_scale * (2.0 * np.pi * signed / R) ** 2
    response = np.fft.ifft(np.exp(-1j * angle))
    shift = np.arange(HALF)[:, None] - np.arange(HALF)[None, :]
    near = response[shift % R]
    far = response[(shift + HALF) % R]
    table = np.zeros((2, 2, HALF // TILE, 2, TILE, HALF), ml_dtypes.bfloat16)
    for i, matrix in enumerate((0.5 * (near + far), 0.5 * (near - far))):
        for c, part in enumerate((matrix.real, matrix.imag)):
            high = part.astype(ml_dtypes.bfloat16)
            low = (part - high.astype(np.float64)).astype(ml_dtypes.bfloat16)
            table[i, 0, :, c] = high.reshape(HALF // TILE, TILE, HALF)
            table[i, 1, :, c] = low.reshape(HALF // TILE, TILE, HALF)
    return table.reshape(2, 2, HALF // TILE, 2 * TILE, HALF)


def split(value):
    high = value.astype(BF16)
    low = (value - high.astype(F32)).astype(BF16)
    return high, low


def take(ref, sem):
    pltpu.make_async_copy(ref, ref, sem).wait()


def kernel(
    x_ref, weight_ref, tiles_ref, list_ref, coupling_ref, table_ref, out_ref,
    xin, send1, recv1a, recv1b, ub, table, ya, yb, recv2a, recv2b,
    tiles, tile_rhs, lhs, sums, adv, rwx, rwb, cpl, send3a, send3b, recv3a, recv3b, res,
    rank, order, src, wrow, same, last,
    xsem, ksem, tsem, ssem1, rsem1, ssem2, rsem2, ssem3, rsem3, wsem, osem,
):
    recv1, yy, recv2 = (recv1a, recv1b), (ya, yb), (recv2a, recv2b)
    send3, recv3 = (send3a, send3b), (recv3a, recv3b)
    zlo = lax.axis_index("hel")
    rad = lax.axis_index("rad")
    core = rad % 2
    x = (rad // 2) % 4
    y = (rad // 8) % 4
    zhi = rad // 32
    z = zhi * 4 + zlo
    q0 = rad % 32
    kap = (x + y) % 4
    cb0 = y * 2 + core

    for p in range(2):
        for part in range(2):
            i = part * 2 + p
            for cb in range(CB):
                pltpu.make_async_copy(
                    x_ref.at[i, :, pl.ds(cb * TILE, TILE)], xin.at[i, cb], xsem.at[i]
                ).start()
    table_copy = pltpu.make_async_copy(table_ref, table, ksem)
    tiles_copy = pltpu.make_async_copy(tiles_ref, tiles, tsem)

    barrier = pltpu.get_barrier_semaphore()

    @pl.loop(0, 64)
    def _(i):
        r = (rad + i) % 64

        @pl.when(jnp.logical_or(r != rad, kap != zlo))
        def _():
            pl.semaphore_signal(barrier, 1, device_id=(kap, r), device_id_type=MESH)

    @pl.loop(1, 8)
    def _(i):
        zz = (z + i) % 8
        pl.semaphore_signal(
            barrier, 1, device_id=(zz % 4, zz // 4 * 32 + q0), device_id_type=MESH
        )

    @pl.loop(1, 32)
    def _(i):
        q = (rad + i) % 32
        pl.semaphore_signal(barrier, 1, device_id=(zlo, zhi * 32 + q), device_id_type=MESH)

    def pack(p):
        for part in range(2):
            i = part * 2 + p
            take(xin.at[i], xsem.at[i])
            for cb in range(CB):
                for v in range(V):
                    send1[p, v, cb, part] = xin[i, cb, pl.ds(v, 16, stride=8), :]

    def scatter_columns(p):
        @pl.loop(0, 64)
        def _(i):
            v = (z + i + 4) % 8
            cb = (y * 2 + core + i // 8 + i) % 8
            dy = cb // 2
            dx = (zlo - dy + 4) % 4
            hel = v % 4
            r = ((v // 4 * 4 + dy) * 4 + dx) * 2 + cb % 2
            source = send1.at[p, v, cb]
            target = recv1[p].at[:, pl.ds(pl.multiple_of(rad * 16, 16), 16), :]
            own = jnp.logical_and(hel == zlo, r == rad)

            @pl.when(own)
            def _():
                pltpu.make_async_copy(source, target, rsem1.at[p]).start()

            @pl.when(jnp.logical_not(own))
            def _():
                pltpu.make_async_remote_copy(
                    source, target, ssem1.at[p], rsem1.at[p],
                    device_id=(hel, r), device_id_type=MESH,
                ).start()

    pack(0)
    pl.semaphore_wait(barrier, 102 - jnp.where(kap == zlo, 1, 0))
    scatter_columns(0)
    pack(1)
    scatter_columns(1)
    table_copy.start()
    tiles_copy.start()

    rwx[zhi] = jnp.zeros((Q, TILE), F32)
    rwx[zhi, :, 0:16] = weight_ref[...]
    weight_copy = pltpu.make_async_remote_copy(
        rwx.at[zhi], rwx.at[zhi], wsem.at[0], wsem.at[1],
        device_id=(zlo, (1 - zhi) * 32 + q0), device_id_type=MESH,
    )
    weight_copy.start()

    @pl.loop(0, NT)
    def _(t):
        mine = list_ref[t, 0]
        count = jnp.int32(0)
        for other in range(NT):
            theirs = list_ref[other, 0]
            ahead = jnp.where(theirs < mine, 1, 0)
            tied = jnp.where(theirs == mine, jnp.where(other < t, 1, 0), 0)
            count = count + ahead + tied
        rank[t] = count

    @pl.loop(0, NT)
    def _(position):
        tile = jnp.int32(0)
        for t in range(NT):
            tile = tile + jnp.where(rank[t] == position, t, 0)
        order[position] = tile
        src[position] = list_ref[tile, 1]
        wrow[position] = list_ref[tile, 2]
        before = order[jnp.maximum(position - 1, 0)]
        same[position] = jnp.where(
            list_ref[tile, 0] == list_ref[before, 0], jnp.where(position > 0, 1, 0), 0
        )

    @pl.loop(0, CB)
    def _(i):
        count = jnp.int32(0)
        for t in range(NT):
            count = count + jnp.where(list_ref[t, 0] <= i, 1, 0)
        last[i] = count

    for cb in range(CB):
        cpl[cb] = coupling_ref[:, cb * TILE:(cb + 1) * TILE]
    sums[0] = jnp.zeros((256, TILE), F32)
    tiles_copy.wait()

    @pl.loop(0, NT)
    def _(position):
        high, low = split(tiles[order[position]])
        tile_rhs[position, 0:TILE] = high
        tile_rhs[position, TILE:2 * TILE] = high
        tile_rhs[position, 2 * TILE:] = low

    weight_copy.wait()
    eye = (
        lax.broadcasted_iota(jnp.int32, (16, 16), 0) == lax.broadcasted_iota(jnp.int32, (16, 16), 1)
    )
    for half in range(2):
        for w in range(Q):
            row = jnp.broadcast_to(rwx[half, w:w + 1, 0:16], (16, 16))
            column = jnp.sum(jnp.where(eye, row, 0.0), axis=1, keepdims=True)
            spread = jnp.broadcast_to(column, (16, TILE))
            rwb[0, w, half * 8:half * 8 + 8] = spread[:8]
            rwb[1, w, half * 8:half * 8 + 8] = spread[8:]
    table_copy.wait()

    for p in range(2):
        take(recv1[p], rsem1.at[p])

        @pl.loop(0, 8)
        def _(i):
            rows = pl.ds(pl.multiple_of(i * 64, 64), 64)
            rows_far = pl.ds(pl.multiple_of(HALF + i * 64, 64), 64)
            for part in range(2):
                near = recv1[p][part, rows, :]
                far = recv1[p][part, rows_far, :]
                for s, value in enumerate((near + far, near - far)):
                    high, low = split(value)
                    ub[s, 0, rows, part * TILE:(part + 1) * TILE] = high
                    ub[s, 1, rows, part * TILE:(part + 1) * TILE] = low

        @pl.loop(0, HALF // TILE)
        def _(block):
            products = []
            for s in range(2):
                total = jnp.dot(table[s, 0, block], ub[s, 0], preferred_element_type=F32)
                total += jnp.dot(table[s, 1, block], ub[s, 0], preferred_element_type=F32)
                total += jnp.dot(table[s, 0, block], ub[s, 1], preferred_element_type=F32)
                real = total[:TILE, :TILE] - total[TILE:, TILE:]
                imag = total[:TILE, TILE:] + total[TILE:, :TILE]
                products.append((real, imag))
            rows = pl.ds(pl.multiple_of(block * TILE, TILE), TILE)
            for part in range(2):
                yy[p][part, 0, rows, :] = products[0][part] + products[1][part]
                yy[p][part, 1, rows, :] = products[0][part] - products[1][part]

        for j in range(2):
            @pl.loop(0, 32)
            def _(i):
                dx = (x + i + y) % 4
                dy = (y + i // 4 + x * 3) % 4
                dc = (core + i // 16 + x + y) % 2
                q = (dy * 4 + dx) * 2 + dc
                source = yy[p].at[:, :, pl.ds(pl.multiple_of(q * 16 + j * 8, 8), 8), :]
                target = recv2[j].at[cb0, :, kap * 2 + p]

                @pl.when(q == q0)
                def _():
                    pltpu.make_async_copy(source, target, rsem2.at[j]).start()

                @pl.when(q != q0)
                def _():
                    pltpu.make_async_remote_copy(
                        source, target, ssem2.at[p], rsem2.at[j],
                        device_id=(zlo, zhi * 32 + q), device_id_type=MESH,
                    ).start()

    for j in range(2):
        field = recv2[j]
        take(field, rsem2.at[j])
        point = lax.broadcasted_iota(jnp.int32, (16, TILE), 0)
        distance = (
            point // 8 * HALF + point % 8 + (q0 * 16 + j * 8)
        ).astype(F32)
        radial_factor = 1.0 / (1.0 + 3.0 * distance / R) ** 2

        def to_lhs(cb, value):
            high, low = split(value)
            lhs[cb, :, 0:TILE] = high
            lhs[cb, :, TILE:2 * TILE] = low
            lhs[cb, :, 2 * TILE:] = high

        @pl.loop(0, CB)
        def _(cb):
            value = field[cb]
            adv[cb] = value.reshape(256, TILE)
            to_lhs(cb, value.reshape(256, TILE))

        for degree in range(1, TAYLOR + 1):
            @pl.loop(0, NT)
            def _(position):
                product = jnp.dot(
                    lhs[src[position]], tile_rhs[position], preferred_element_type=F32
                )
                scaled = product.reshape(16, 16, TILE) * rwb[j, wrow[position]][None]
                carried = jnp.where(same[position] == 1, sums[position], 0.0)
                sums[position + 1] = scaled.reshape(256, TILE) + carried

            @pl.loop(0, CB)
            def _(cb):
                potential = sums[last[cb]].reshape(2, K, 16, TILE)
                strength = cpl[cb]
                rows = [
                    jnp.broadcast_to(strength[k:k + 1], (16, TILE)) * radial_factor
                    for k in range(K - 1)
                ]
                applied = []
                for part in range(2):
                    w = [field[cb, part, k].reshape(16, TILE) for k in range(K)]
                    for k in range(K):
                        value = potential[part, k]
                        if k + 1 < K:
                            value = value + rows[k] * w[k + 1]
                        if k > 0:
                            value = value + rows[k - 1] * w[k - 1]
                        applied.append(value)
                scale = 1.0 / degree
                term = [a * scale for a in applied[K:]] + [a * -scale for a in applied[:K]]
                if degree < TAYLOR:
                    stacked = jnp.concatenate(term, axis=0)
                    adv[cb] = adv[cb] + stacked
                    to_lhs(cb, stacked)
                    for i in range(2 * K):
                        field[cb, i // K, i % K] = term[i].reshape(2, 8, TILE)
                else:
                    lanes = pl.ds(pl.multiple_of(cb * TILE, TILE), TILE)
                    for i in range(2 * K):
                        part, k = i // K, i % K
                        final = adv[cb, i * 16:(i + 1) * 16] + term[i]
                        for half in range(2):
                            send3[j][half * 4 + k // 2, part, k % 2, :, lanes] = final[
                                half * 8:half * 8 + 8
                            ]

        @pl.loop(0, 8)
        def _(o):
            zz = (z + o * 3 + 4) % 8
            source = send3[j].at[zz]
            target = recv3[j].at[z]

            @pl.when(zz == z)
            def _():
                pltpu.make_async_copy(source, target, rsem3.at[j]).start()

            @pl.when(zz != z)
            def _():
                pltpu.make_async_remote_copy(
                    source, target, ssem3.at[j], rsem3.at[j],
                    device_id=(zz % 4, zz // 4 * 32 + q0), device_id_type=MESH,
                ).start()

    for j in range(2):
        take(recv3[j], rsem3.at[j])
        for i in range(4):
            for cb in range(CB):
                for v in range(V):
                    res[i, cb, pl.ds(j * 64 + v, 8, stride=8), :] = recv3[j][
                        v, i // 2, i % 2, :, cb * TILE:(cb + 1) * TILE
                    ]
                pltpu.make_async_copy(
                    res.at[i, cb, pl.ds(j * 64, 64), :],
                    out_ref.at[i, pl.ds(j * 64, 64), pl.ds(cb * TILE, TILE)],
                    osem,
                ).start()

    take(res, osem)
    for p in range(2):
        @pl.when(kap == zlo)
        def _():
            take(send1.at[p, pl.ds(0, 7)], ssem1.at[p])
            take(send1.at[p, 7, pl.ds(0, 7)], ssem1.at[p])

        @pl.when(kap != zlo)
        def _():
            take(send1.at[p], ssem1.at[p])

        take(yy[p].at[:, :, pl.ds(0, HALF - 16), :], ssem2.at[p])
        take(send3[p].at[pl.ds(0, 7)], ssem3.at[p])


def step(packet, radial_weight, tile_blocks, tile_list, coupling):
    flat = packet.reshape(4, 16 * V, CB * TILE)
    table = jnp.asarray(propagator_tables())
    anywhere = pl.BlockSpec(memory_space=pl.ANY)
    vmem = pl.BlockSpec(memory_space=pltpu.VMEM)
    dma = pltpu.SemaphoreType.DMA
    out = pl.pallas_call(
        kernel,
        out_shape=jax.ShapeDtypeStruct(flat.shape, F32),
        in_specs=[
            anywhere, vmem, anywhere, pl.BlockSpec(memory_space=pltpu.SMEM), vmem, anywhere,
        ],
        out_specs=anywhere,
        scratch_shapes=[
            pltpu.VMEM((4, CB, 128, TILE), F32),
            pltpu.VMEM((2, V, CB, 2, 16, TILE), F32),
            pltpu.VMEM((2, R, TILE), F32),
            pltpu.VMEM((2, R, TILE), F32),
            pltpu.VMEM((2, 2, HALF, 2 * TILE), BF16),
            pltpu.VMEM(table.shape, BF16),
            pltpu.VMEM((2, 2, HALF, TILE), F32),
            pltpu.VMEM((2, 2, HALF, TILE), F32),
            pltpu.VMEM((CB, 2, K, 2, 8, TILE), F32),
            pltpu.VMEM((CB, 2, K, 2, 8, TILE), F32),
            pltpu.VMEM((NT, TILE, TILE), F32),
            pltpu.VMEM((NT, 3 * TILE, TILE), BF16),
            pltpu.VMEM((CB, 256, 3 * TILE), BF16),
            pltpu.VMEM((NT + 1, 256, TILE), F32),
            pltpu.VMEM((CB, 256, TILE), F32),
            pltpu.VMEM((2, Q, TILE), F32),
            pltpu.VMEM((2, Q, 16, TILE), F32),
            pltpu.VMEM((CB, K, TILE), F32),
            pltpu.VMEM((8, 2, 2, 8, CB * TILE), F32),
            pltpu.VMEM((8, 2, 2, 8, CB * TILE), F32),
            pltpu.VMEM((8, 2, 2, 8, CB * TILE), F32),
            pltpu.VMEM((8, 2, 2, 8, CB * TILE), F32),
            pltpu.VMEM((4, CB, 128, TILE), F32),
            pltpu.SMEM((NT,), jnp.int32),
            pltpu.SMEM((NT,), jnp.int32),
            pltpu.SMEM((NT,), jnp.int32),
            pltpu.SMEM((NT,), jnp.int32),
            pltpu.SMEM((NT,), jnp.int32),
            pltpu.SMEM((CB,), jnp.int32),
            dma((4,)), dma(()), dma(()),
            dma((2,)), dma((2,)), dma((2,)), dma((2,)), dma((2,)), dma((2,)), dma((2,)), dma(()),
        ],
        compiler_params=pltpu.CompilerParams(
            collective_id=0, has_side_effects=True, vmem_limit_bytes=56 << 20
        ),
        name="wavepacket_step",
    )(flat, radial_weight, tile_blocks, tile_list, coupling, table)
    return out.reshape(packet.shape)


def solution(mesh):
    in_specs = (P(None, "hel", "rad"), P(None, "rad"), P(), P(), P())
    return jax.shard_map(
        step,
        mesh=mesh,
        in_specs=in_specs,
        out_specs=P(None, "hel", "rad"),
        check_vma=False,
    )
```

time: 1150 us -> 155 us (0.13); the launches traced: 1130 us -> 155 us
  loops' own time: 414 us -> 0 us
  local copies, waits for them, and re-layouts: 294 us -> 4.52 us
  matrix products: 247 us -> 0 us
  Pallas kernels: 0 us -> 150 us
  starting transfers between devices: 77.9 us -> 0 us
  waiting for transfers between devices: 69.3 us -> 0 us
  other arithmetic: 27 us -> 0 us
    another operation x3 -> x0, loops' own time: 414 us -> none  [potential(): lax.fori_loop(0, tile_list.shape[0], add_tile, jnp.zeros(blocks.shape, jn...]
    dot_general x76 -> x0, matrix products: 247 us -> none  [the longest x72 144 us: add_tile(): jnp.einsum('ckrvi,ij->ckrvj', source_block, matrix, precision=lax.Precisi...]
    pallas_call x0 -> x1, Pallas kernels: none -> 150 us  [step(): pl.pallas_call(kernel, out_shape=jax.ShapeDtypeStruct(flat.shape, F32), i...]
    dynamic_slice x168 -> x0, local copies, waits for them, and re-layouts: 141 us -> none  [the longest x72 70.1 us: add_tile(): current = lax.dynamic_index_in_dim(summed, target, 4, keepdims=False)]
    all_to_all x2 -> x0, waiting for transfers between devices: 69.3 us -> none  [the longest x1 37.8 us: body(): lax.all_to_all(flattened, 'rad', split_axis=3, concat_axis=2, tiled=True)]
    unnamed x25 -> x2, local copies, waits for them, and re-layouts: 68.9 us -> 4.52 us
    mul x72 -> x0, local copies, waits for them, and re-layouts: 50.1 us -> none  [add_tile(): product = product * factor[None, None, :, None, None]]
    ppermute x6 -> x0, starting transfers between devices: 45.4 us -> none  [the longest x3 41.4 us: extended(): lax.ppermute(lax.slice_in_dim(block, block.shape[dim] - width, None, axis...]
  transfers between devices with their start and end apart: 8 -> 0, of which waited for: 2 -> 0; matrix products, arithmetic and copies ran while one was open for 30% -> 0% of each run, Pallas kernels for 0% -> 0%
where the time goes in v1:
time: 155 us
  Pallas kernels  150 us (97%)
  local copies, waits for them, and re-layouts  4.52 us (3%)
    pallas_call x1, Pallas kernels, step(): pl.pallas_call(kernel, out_shape=jax.ShapeDtypeStruct(flat.shape, F32), i...  150 us
    unnamed x2, local copies, waits for them, and re-layouts  4.52 us

profile of v1, /device:TPU:1, one launch (start us, length us, event | category | flops | bytes accessed | tf_op | source)
XLA Modules:
  0.0 154.9 jit_solution(7926989464034768452)
XLA Ops:
  0.0 1.4 copy.7.list_ref
  1.4 150.4 %wavepacket_step.1 = f32[4,128,1024]{2,1,0:T(8,128)} custom-call(f32[4,128,1024]{2,1,0:T(8,128)} %bitcast.3, f32[8,16]{1,0:T(8,128)} %weight_ref.1, f32[24,128,128]{2,1,0:T(8,128)} %tiles_ref.1, s32[24,3]{1,0:T(8,128)} %copy.7.list_ref, f32[8,1024]{1,0:T(8,128)} %coupling_ref.1, bf16[2,2,4,256,512]{4,3,2,1,0:T(8,128)(2,1)} %constant.2.clone.table_ref), custom_call_target="tpu_custom_call" | custom-call | tf_op jit(solution)/shard_map/wavepacket_step/pallas_call | solution.py:382
  151.8 3.2 %copy.9 = f32[2,2,16,8,1024]{4,3,2,1,0:T(8,128)} copy(f32[2,2,16,8,1024]{4,3,2,1,0:T(8,128)} %bitcast.2) | data formatting | bytes 4194304

commit v2 on v1

--- a/solution.py
+++ b/solution.py
@@ -113,8 +113,8 @@
                 for v in range(V):
                     send1[p, v, cb, part] = xin[i, cb, pl.ds(v, 16, stride=8), :]
 
-    def scatter_columns(p):
-        @pl.loop(0, 64)
+    def scatter_columns(p, h):
+        @pl.loop(h * 32, h * 32 + 32)
         def _(i):
             v = (z + i + 4) % 8
             cb = (y * 2 + core + i // 8 + i) % 8
@@ -133,15 +133,29 @@
             @pl.when(jnp.logical_not(own))
             def _():
                 pltpu.make_async_remote_copy(
-                    source, target, ssem1.at[p], rsem1.at[p],
+                    source, target, ssem1.at[2 * p + h], rsem1.at[p],
                     device_id=(hel, r), device_id_type=MESH,
                 ).start()
 
+    def scattered(p, h):
+        if h == 0:
+            take(send1.at[p, pl.ds(0, 4)], ssem1.at[2 * p])
+            return
+
+        @pl.when(kap == zlo)
+        def _():
+            take(send1.at[p, pl.ds(0, 3)], ssem1.at[2 * p + 1])
+            take(send1.at[p, 3, pl.ds(0, 7)], ssem1.at[2 * p + 1])
+
+        @pl.when(kap != zlo)
+        def _():
+            take(send1.at[p, pl.ds(0, 4)], ssem1.at[2 * p + 1])
+
     pack(0)
     pl.semaphore_wait(barrier, 102 - jnp.where(kap == zlo, 1, 0))
-    scatter_columns(0)
+    scatter_columns(0, 0)
+    scatter_columns(0, 1)
     pack(1)
-    scatter_columns(1)
     table_copy.start()
     tiles_copy.start()
 
@@ -153,12 +167,17 @@
     )
     weight_copy.start()
 
+    scattered(0, 0)
+    scatter_columns(1, 0)
+    scattered(0, 1)
+    scatter_columns(1, 1)
+
     @pl.loop(0, NT)
     def _(t):
-        mine = list_ref[t, 0]
+        mine = list_ref[0, t]
         count = jnp.int32(0)
         for other in range(NT):
-            theirs = list_ref[other, 0]
+            theirs = list_ref[0, other]
             ahead = jnp.where(theirs < mine, 1, 0)
             tied = jnp.where(theirs == mine, jnp.where(other < t, 1, 0), 0)
             count = count + ahead + tied
@@ -170,18 +189,18 @@
         for t in range(NT):
             tile = tile + jnp.where(rank[t] == position, t, 0)
         order[position] = tile
-        src[position] = list_ref[tile, 1]
-        wrow[position] = list_ref[tile, 2]
+        src[position] = list_ref[1, tile]
+        wrow[position] = list_ref[2, tile]
         before = order[jnp.maximum(position - 1, 0)]
         same[position] = jnp.where(
-            list_ref[tile, 0] == list_ref[before, 0], jnp.where(position > 0, 1, 0), 0
+            list_ref[0, tile] == list_ref[0, before], jnp.where(position > 0, 1, 0), 0
         )
 
     @pl.loop(0, CB)
     def _(i):
         count = jnp.int32(0)
         for t in range(NT):
-            count = count + jnp.where(list_ref[t, 0] <= i, 1, 0)
+            count = count + jnp.where(list_ref[0, t] <= i, 1, 0)
         last[i] = count
 
     for cb in range(CB):
@@ -282,7 +301,7 @@
             to_lhs(cb, value.reshape(256, TILE))
 
         for degree in range(1, TAYLOR + 1):
-            @pl.loop(0, NT)
+            @pl.loop(0, NT, unroll=NT)
             def _(position):
                 product = jnp.dot(
                     lhs[src[position]], tile_rhs[position], preferred_element_type=F32
@@ -359,16 +378,9 @@
                 ).start()
 
     take(res, osem)
+    scattered(1, 0)
+    scattered(1, 1)
     for p in range(2):
-        @pl.when(kap == zlo)
-        def _():
-            take(send1.at[p, pl.ds(0, 7)], ssem1.at[p])
-            take(send1.at[p, 7, pl.ds(0, 7)], ssem1.at[p])
-
-        @pl.when(kap != zlo)
-        def _():
-            take(send1.at[p], ssem1.at[p])
-
         take(yy[p].at[:, :, pl.ds(0, HALF - 16), :], ssem2.at[p])
         take(send3[p].at[pl.ds(0, 7)], ssem3.at[p])
 
@@ -417,13 +429,13 @@
             pltpu.SMEM((NT,), jnp.int32),
             pltpu.SMEM((CB,), jnp.int32),
             dma((4,)), dma(()), dma(()),
-            dma((2,)), dma((2,)), dma((2,)), dma((2,)), dma((2,)), dma((2,)), dma((2,)), dma(()),
+            dma((4,)), dma((2,)), dma((2,)), dma((2,)), dma((2,)), dma((2,)), dma((2,)), dma(()),
         ],
         compiler_params=pltpu.CompilerParams(
             collective_id=0, has_side_effects=True, vmem_limit_bytes=56 << 20
         ),
         name="wavepacket_step",
-    )(flat, radial_weight, tile_blocks, tile_list, coupling, table)
+    )(flat, radial_weight, tile_blocks, tile_list.T, coupling, table)
     return out.reshape(packet.shape)
 
 

time: 155 us -> 132 us (0.85)
  Pallas kernels: 150 us -> 129 us
    pallas_call x1, Pallas kernels: 150 us -> 129 us  [step(): pl.pallas_call(kernel, out_shape=jax.ShapeDtypeStruct(flat.shape, F32), i...]
    unnamed x2 -> x1, local copies, waits for them, and re-layouts: 4.52 us -> 3.16 us
where the time goes in v2:
time: 132 us
  Pallas kernels  129 us (98%)
  local copies, waits for them, and re-layouts  3.16 us (2%)
    pallas_call x1, Pallas kernels, step(): pl.pallas_call(kernel, out_shape=jax.ShapeDtypeStruct(flat.shape, F32), i...  129 us
    unnamed x1, local copies, waits for them, and re-layouts  3.16 us

profile of v2, /device:TPU:1, one launch (start us, length us, event | category | flops | bytes accessed | tf_op | source)
XLA Modules:
  0.0 131.8 jit_solution(1159067410464721780)
XLA Ops:
  0.0 128.6 %wavepacket_step.1 = f32[4,128,1024]{2,1,0:T(8,128)} custom-call(f32[4,128,1024]{2,1,0:T(8,128)} %bitcast.4, f32[8,16]{1,0:T(8,128)} %weight_ref.1, f32[24,128,128]{2,1,0:T(8,128)} %tiles_ref.1, s32[3,24]{1,0:T(4,128)} %bitcast.5, f32[8,1024]{1,0:T(8,128)} %coupling_ref.1, bf16[2,2,4,256,512]{4,3,2,1,0:T(8,128)(2,1)} %constant.2.clone.table_ref), custom_call_target="tpu_custom_call" | custom-call | tf_op jit(solution)/shard_map/wavepacket_step/pallas_call | solution.py:394
  128.6 3.2 %copy.8 = f32[2,2,16,8,1024]{4,3,2,1,0:T(8,128)} copy(f32[2,2,16,8,1024]{4,3,2,1,0:T(8,128)} %bitcast.3) | data formatting | bytes 4194304

commit v3 on v2

--- a/solution.py
+++ b/solution.py
@@ -30,7 +30,8 @@
     signed = np.where(wave < R // 2, wave, wave - R).astype(np.float64)
     angle = kinetic_scale * (2.0 * np.pi * signed / R) ** 2
     response = np.fft.ifft(np.exp(-1j * angle))
-    shift = np.arange(HALF)[:, None] - np.arange(HALF)[None, :]
+    rows = np.arange(HALF).reshape(32, 2, 8).transpose(1, 0, 2).reshape(HALF)
+    shift = rows[:, None] - np.arange(HALF)[None, :]
     near = response[shift % R]
     far = response[(shift + HALF) % R]
     table = np.zeros((2, 2, HALF // TILE, 2, TILE, HALF), ml_dtypes.bfloat16)
@@ -55,13 +56,12 @@
 
 def kernel(
     x_ref, weight_ref, tiles_ref, list_ref, coupling_ref, table_ref, out_ref,
-    xin, send1, recv1a, recv1b, ub, table, ya, yb, recv2a, recv2b,
-    tiles, tile_rhs, lhs, sums, adv, rwx, rwb, cpl, send3a, send3b, recv3a, recv3b, res,
+    xin, send1, recv1a, recv1b, ub, table, ya, yb, recv2,
+    tiles, tile_rhs, lhs, sums, adv, rwx, rwb, cpl, send3, recv3a, recv3b, res,
     rank, order, src, wrow, same, last,
     xsem, ksem, tsem, ssem1, rsem1, ssem2, rsem2, ssem3, rsem3, wsem, osem,
 ):
-    recv1, yy, recv2 = (recv1a, recv1b), (ya, yb), (recv2a, recv2b)
-    send3, recv3 = (send3a, send3b), (recv3a, recv3b)
+    recv1, yy, recv3 = (recv1a, recv1b), (ya, yb), (recv3a, recv3b)
     zlo = lax.axis_index("hel")
     rad = lax.axis_index("rad")
     core = rad % 2
@@ -205,7 +205,7 @@
 
     for cb in range(CB):
         cpl[cb] = coupling_ref[:, cb * TILE:(cb + 1) * TILE]
-    sums[0] = jnp.zeros((256, TILE), F32)
+    sums[0] = jnp.zeros((TILE, TILE), F32)
     tiles_copy.wait()
 
     @pl.loop(0, NT)
@@ -224,9 +224,31 @@
             row = jnp.broadcast_to(rwx[half, w:w + 1, 0:16], (16, 16))
             column = jnp.sum(jnp.where(eye, row, 0.0), axis=1, keepdims=True)
             spread = jnp.broadcast_to(column, (16, TILE))
-            rwb[0, w, half * 8:half * 8 + 8] = spread[:8]
-            rwb[1, w, half * 8:half * 8 + 8] = spread[8:]
+            rwb[half, 0, w] = spread[:8]
+            rwb[half, 1, w] = spread[8:]
     table_copy.wait()
+
+    def gather_points(p, c):
+        @pl.loop(0, 32)
+        def _(i):
+            dx = (x + i + y) % 4
+            dy = (y + i // 4 + x * 3) % 4
+            dc = (core + i // 16 + x + y) % 2
+            q = (dy * 4 + dx) * 2 + dc
+            rows = pl.ds(pl.multiple_of(q * 8, 8), 8)
+            source = yy[p].at[:, (zhi + 1 - c // 2) % 2, c % 2, rows, :]
+            target = recv2.at[c, cb0, :, kap * 2 + p]
+
+            @pl.when(q == q0)
+            def _():
+                pltpu.make_async_copy(source, target, rsem2.at[c]).start()
+
+            @pl.when(q != q0)
+            def _():
+                pltpu.make_async_remote_copy(
+                    source, target, ssem2.at[c if p else 4], rsem2.at[c],
+                    device_id=(zlo, zhi * 32 + q), device_id_type=MESH,
+                ).start()
 
     for p in range(2):
         take(recv1[p], rsem1.at[p])
@@ -243,49 +265,39 @@
                     ub[s, 0, rows, part * TILE:(part + 1) * TILE] = high
                     ub[s, 1, rows, part * TILE:(part + 1) * TILE] = low
 
-        @pl.loop(0, HALF // TILE)
-        def _(block):
-            products = []
-            for s in range(2):
-                total = jnp.dot(table[s, 0, block], ub[s, 0], preferred_element_type=F32)
-                total += jnp.dot(table[s, 1, block], ub[s, 0], preferred_element_type=F32)
-                total += jnp.dot(table[s, 0, block], ub[s, 1], preferred_element_type=F32)
-                real = total[:TILE, :TILE] - total[TILE:, TILE:]
-                imag = total[:TILE, TILE:] + total[TILE:, :TILE]
-                products.append((real, imag))
-            rows = pl.ds(pl.multiple_of(block * TILE, TILE), TILE)
-            for part in range(2):
-                yy[p][part, 0, rows, :] = products[0][part] + products[1][part]
-                yy[p][part, 1, rows, :] = products[0][part] - products[1][part]
-
         for j in range(2):
-            @pl.loop(0, 32)
+            @pl.loop(0, 2)
             def _(i):
-                dx = (x + i + y) % 4
-                dy = (y + i // 4 + x * 3) % 4
-                dc = (core + i // 16 + x + y) % 2
-                q = (dy * 4 + dx) * 2 + dc
-                source = yy[p].at[:, :, pl.ds(pl.multiple_of(q * 16 + j * 8, 8), 8), :]
-                target = recv2[j].at[cb0, :, kap * 2 + p]
-
-                @pl.when(q == q0)
-                def _():
-                    pltpu.make_async_copy(source, target, rsem2.at[j]).start()
-
-                @pl.when(q != q0)
-                def _():
-                    pltpu.make_async_remote_copy(
-                        source, target, ssem2.at[p], rsem2.at[j],
-                        device_id=(zlo, zhi * 32 + q), device_id_type=MESH,
-                    ).start()
-
-    for j in range(2):
-        field = recv2[j]
-        take(field, rsem2.at[j])
-        point = lax.broadcasted_iota(jnp.int32, (16, TILE), 0)
-        distance = (
-            point // 8 * HALF + point % 8 + (q0 * 16 + j * 8)
-        ).astype(F32)
+                block = j * 2 + i
+                products = []
+                for s in range(2):
+                    total = jnp.dot(table[s, 0, block], ub[s, 0], preferred_element_type=F32)
+                    total += jnp.dot(table[s, 1, block], ub[s, 0], preferred_element_type=F32)
+                    total += jnp.dot(table[s, 0, block], ub[s, 1], preferred_element_type=F32)
+                    real = total[:TILE, :TILE] - total[TILE:, TILE:]
+                    imag = total[:TILE, TILE:] + total[TILE:, :TILE]
+                    products.append((real, imag))
+                rows = pl.ds(pl.multiple_of(i * TILE, TILE), TILE)
+                for part in range(2):
+                    yy[p][part, 0, j, rows, :] = products[0][part] + products[1][part]
+                    yy[p][part, 1, j, rows, :] = products[0][part] - products[1][part]
+
+            for c in ((j, j + 2) if p == 0 else (0,) if j == 0 else ()):
+                gather_points(p, c)
+
+    @pl.loop(0, 4)
+    def _(c):
+        half = (zhi + 1 - c // 2) % 2
+        j = c % 2
+        take(yb.at[:, 0, 0, pl.ds(0, 248), :], ssem2.at[c])
+
+        @pl.when(c < 3)
+        def _():
+            gather_points(1, c + 1)
+
+        take(recv2.at[c], rsem2.at[c])
+        point = lax.broadcasted_iota(jnp.int32, (8, TILE), 0)
+        distance = (point + (half * HALF + q0 * 16 + j * 8)).astype(F32)
         radial_factor = 1.0 / (1.0 + 3.0 * distance / R) ** 2
 
         def to_lhs(cb, value):
@@ -296,9 +308,9 @@
 
         @pl.loop(0, CB)
         def _(cb):
-            value = field[cb]
-            adv[cb] = value.reshape(256, TILE)
-            to_lhs(cb, value.reshape(256, TILE))
+            value = recv2[c, cb].reshape(TILE, TILE)
+            adv[cb] = value
+            to_lhs(cb, value)
 
         for degree in range(1, TAYLOR + 1):
             @pl.loop(0, NT, unroll=NT)
@@ -306,21 +318,21 @@
                 product = jnp.dot(
                     lhs[src[position]], tile_rhs[position], preferred_element_type=F32
                 )
-                scaled = product.reshape(16, 16, TILE) * rwb[j, wrow[position]][None]
+                scaled = product.reshape(16, 8, TILE) * rwb[half, j, wrow[position]][None]
                 carried = jnp.where(same[position] == 1, sums[position], 0.0)
-                sums[position + 1] = scaled.reshape(256, TILE) + carried
+                sums[position + 1] = scaled.reshape(TILE, TILE) + carried
 
             @pl.loop(0, CB)
             def _(cb):
-                potential = sums[last[cb]].reshape(2, K, 16, TILE)
+                potential = sums[last[cb]].reshape(2, K, 8, TILE)
                 strength = cpl[cb]
                 rows = [
-                    jnp.broadcast_to(strength[k:k + 1], (16, TILE)) * radial_factor
+                    jnp.broadcast_to(strength[k:k + 1], (8, TILE)) * radial_factor
                     for k in range(K - 1)
                 ]
                 applied = []
                 for part in range(2):
-                    w = [field[cb, part, k].reshape(16, TILE) for k in range(K)]
+                    w = [recv2[c, cb, part, k] for k in range(K)]
                     for k in range(K):
                         value = potential[part, k]
                         if k + 1 < K:
@@ -335,33 +347,31 @@
                     adv[cb] = adv[cb] + stacked
                     to_lhs(cb, stacked)
                     for i in range(2 * K):
-                        field[cb, i // K, i % K] = term[i].reshape(2, 8, TILE)
+                        recv2[c, cb, i // K, i % K] = term[i]
                 else:
                     lanes = pl.ds(pl.multiple_of(cb * TILE, TILE), TILE)
                     for i in range(2 * K):
                         part, k = i // K, i % K
-                        final = adv[cb, i * 16:(i + 1) * 16] + term[i]
-                        for half in range(2):
-                            send3[j][half * 4 + k // 2, part, k % 2, :, lanes] = final[
-                                half * 8:half * 8 + 8
-                            ]
-
-        @pl.loop(0, 8)
+                        send3[c, k // 2, part, k % 2, :, lanes] = adv[cb, i * 8:(i + 1) * 8] + term[i]
+
+        @pl.loop(0, 4)
         def _(o):
-            zz = (z + o * 3 + 4) % 8
-            source = send3[j].at[zz]
-            target = recv3[j].at[z]
-
-            @pl.when(zz == z)
-            def _():
-                pltpu.make_async_copy(source, target, rsem3.at[j]).start()
-
-            @pl.when(zz != z)
-            def _():
-                pltpu.make_async_remote_copy(
-                    source, target, ssem3.at[j], rsem3.at[j],
-                    device_id=(zz % 4, zz // 4 * 32 + q0), device_id_type=MESH,
-                ).start()
+            pair = (zlo + o) % 4
+            source = send3.at[c, pair]
+            for jj in range(2):
+                target = recv3[jj].at[z]
+                own = jnp.logical_and(pair == zlo, c >= 2)
+
+                @pl.when(jnp.logical_and(own, j == jj))
+                def _():
+                    pltpu.make_async_copy(source, target, rsem3.at[jj]).start()
+
+                @pl.when(jnp.logical_and(jnp.logical_not(own), j == jj))
+                def _():
+                    pltpu.make_async_remote_copy(
+                        source, target, ssem3.at[c], rsem3.at[jj],
+                        device_id=(pair, half * 32 + q0), device_id_type=MESH,
+                    ).start()
 
     for j in range(2):
         take(recv3[j], rsem3.at[j])
@@ -380,9 +390,9 @@
     take(res, osem)
     scattered(1, 0)
     scattered(1, 1)
-    for p in range(2):
-        take(yy[p].at[:, :, pl.ds(0, HALF - 16), :], ssem2.at[p])
-        take(send3[p].at[pl.ds(0, 7)], ssem3.at[p])
+    take(ya.at[:, :, :, pl.ds(0, 248), :], ssem2.at[4])
+    for c in range(4):
+        take(send3.at[c, pl.ds(0, 4 if c < 2 else 3)], ssem3.at[c])
 
 
 def step(packet, radial_weight, tile_blocks, tile_list, coupling):
@@ -405,20 +415,18 @@
             pltpu.VMEM((2, R, TILE), F32),
             pltpu.VMEM((2, 2, HALF, 2 * TILE), BF16),
             pltpu.VMEM(table.shape, BF16),
-            pltpu.VMEM((2, 2, HALF, TILE), F32),
-            pltpu.VMEM((2, 2, HALF, TILE), F32),
-            pltpu.VMEM((CB, 2, K, 2, 8, TILE), F32),
-            pltpu.VMEM((CB, 2, K, 2, 8, TILE), F32),
+            pltpu.VMEM((2, 2, 2, HALF // 2, TILE), F32),
+            pltpu.VMEM((2, 2, 2, HALF // 2, TILE), F32),
+            pltpu.VMEM((4, CB, 2, K, 8, TILE), F32),
             pltpu.VMEM((NT, TILE, TILE), F32),
             pltpu.VMEM((NT, 3 * TILE, TILE), BF16),
-            pltpu.VMEM((CB, 256, 3 * TILE), BF16),
-            pltpu.VMEM((NT + 1, 256, TILE), F32),
-            pltpu.VMEM((CB, 256, TILE), F32),
+            pltpu.VMEM((CB, TILE, 3 * TILE), BF16),
+            pltpu.VMEM((NT + 1, TILE, TILE), F32),
+            pltpu.VMEM((CB, TILE, TILE), F32),
             pltpu.VMEM((2, Q, TILE), F32),
-            pltpu.VMEM((2, Q, 16, TILE), F32),
+            pltpu.VMEM((2, 2, Q, 8, TILE), F32),
             pltpu.VMEM((CB, K, TILE), F32),
-            pltpu.VMEM((8, 2, 2, 8, CB * TILE), F32),
-            pltpu.VMEM((8, 2, 2, 8, CB * TILE), F32),
+            pltpu.VMEM((4, 4, 2, 2, 8, CB * TILE), F32),
             pltpu.VMEM((8, 2, 2, 8, CB * TILE), F32),
             pltpu.VMEM((8, 2, 2, 8, CB * TILE), F32),
             pltpu.VMEM((4, CB, 128, TILE), F32),
@@ -429,7 +437,7 @@
             pltpu.SMEM((NT,), jnp.int32),
             pltpu.SMEM((CB,), jnp.int32),
             dma((4,)), dma(()), dma(()),
-            dma((4,)), dma((2,)), dma((2,)), dma((2,)), dma((2,)), dma((2,)), dma((2,)), dma(()),
+            dma((4,)), dma((2,)), dma((5,)), dma((4,)), dma((4,)), dma((2,)), dma((2,)), dma(()),
         ],
         compiler_params=pltpu.CompilerParams(
             collective_id=0, has_side_effects=True, vmem_limit_bytes=56 << 20

time: 132 us -> 126 us (0.955)
  Pallas kernels: 129 us -> 122 us
    pallas_call x1, Pallas kernels: 129 us -> 122 us  [step(): pl.pallas_call(kernel, out_shape=jax.ShapeDtypeStruct(flat.shape, F32), i...]
where the time goes in v3:
time: 126 us; the launch traced here: 125 us
  Pallas kernels  122 us (97%)
  local copies, waits for them, and re-layouts  3.16 us (3%)
    pallas_call x1, Pallas kernels, step(): pl.pallas_call(kernel, out_shape=jax.ShapeDtypeStruct(flat.shape, F32), i...  122 us
    unnamed x1, local copies, waits for them, and re-layouts  3.16 us

profile of v3, /device:TPU:1, one launch (start us, length us, event | category | flops | bytes accessed | tf_op | source)
XLA Modules:
  0.0 125.3 jit_solution(15294136103895272192)
XLA Ops:
  0.0 122.1 %wavepacket_step.1 = f32[4,128,1024]{2,1,0:T(8,128)} custom-call(f32[4,128,1024]{2,1,0:T(8,128)} %bitcast.4, f32[8,16]{1,0:T(8,128)} %weight_ref.1, f32[24,128,128]{2,1,0:T(8,128)} %tiles_ref.1, s32[3,24]{1,0:T(4,128)} %bitcast.5, f32[8,1024]{1,0:T(8,128)} %coupling_ref.1, bf16[2,2,4,256,512]{4,3,2,1,0:T(8,128)(2,1)} %constant.2.clone.table_ref), custom_call_target="tpu_custom_call" | custom-call | tf_op jit(solution)/shard_map/wavepacket_step/pallas_call | solution.py:404
  122.1 3.2 %copy.8 = f32[2,2,16,8,1024]{4,3,2,1,0:T(8,128)} copy(f32[2,2,16,8,1024]{4,3,2,1,0:T(8,128)} %bitcast.3) | data formatting | bytes 4194304

commit v4 on v3

--- a/solution.py
+++ b/solution.py
@@ -116,7 +116,7 @@
     def scatter_columns(p, h):
         @pl.loop(h * 32, h * 32 + 32)
         def _(i):
-            v = (z + i + 4) % 8
+            v = (z + i * (1 + 6 * core) + 4) % 8
             cb = (y * 2 + core + i // 8 + i) % 8
             dy = cb // 2
             dx = (zlo - dy + 4) % 4
@@ -403,11 +403,11 @@
     dma = pltpu.SemaphoreType.DMA
     out = pl.pallas_call(
         kernel,
-        out_shape=jax.ShapeDtypeStruct(flat.shape, F32),
+        out_shape=pltpu.VMEM(flat.shape, F32),
         in_specs=[
             anywhere, vmem, anywhere, pl.BlockSpec(memory_space=pltpu.SMEM), vmem, anywhere,
         ],
-        out_specs=anywhere,
+        out_specs=vmem,
         scratch_shapes=[
             pltpu.VMEM((4, CB, 128, TILE), F32),
             pltpu.VMEM((2, V, CB, 2, 16, TILE), F32),
@@ -440,7 +440,7 @@
             dma((4,)), dma((2,)), dma((5,)), dma((4,)), dma((4,)), dma((2,)), dma((2,)), dma(()),
         ],
         compiler_params=pltpu.CompilerParams(
-            collective_id=0, has_side_effects=True, vmem_limit_bytes=56 << 20
+            collective_id=0, has_side_effects=True, vmem_limit_bytes=60 << 20
         ),
         name="wavepacket_step",
     )(flat, radial_weight, tile_blocks, tile_list.T, coupling, table)

time: 126 us -> 123 us (0.976)
  local copies, waits for them, and re-layouts: 3.16 us -> 1.32 us
    unnamed x1, local copies, waits for them, and re-layouts: 3.16 us -> 1.32 us
where the time goes in v4:
time: 123 us
  Pallas kernels  122 us (99%)
  local copies, waits for them, and re-layouts  1.32 us (1%)
    pallas_call x1, Pallas kernels, step(): pl.pallas_call(kernel, out_shape=pltpu.VMEM(flat.shape, F32), in_specs=[a...  122 us

profile of v4, /device:TPU:1, one launch (start us, length us, event | category | flops | bytes accessed | tf_op | source)
XLA Modules:
  0.0 123.0 jit_solution(1475376714181660958)
XLA Ops:
  0.0 121.6 %wavepacket_step.1 = f32[4,128,1024]{2,1,0:T(8,128)S(1)} custom-call(f32[4,128,1024]{2,1,0:T(8,128)} %bitcast.4, f32[8,16]{1,0:T(8,128)} %weight_ref.1, f32[24,128,128]{2,1,0:T(8,128)} %tiles_ref.1, s32[3,24]{1,0:T(4,128)} %bitcast.5, f32[8,1024]{1,0:T(8,128)} %coupling_ref.1, bf16[2,2,4,256,512]{4,3,2,1,0:T(8,128)(2,1)} %constant.2.clone.table_ref), custom_call_target="tpu_custom_call" | custom-call | tf_op jit(solution)/shard_map/wavepacket_step/pallas_call | solution.py:404
  121.6 1.3 %copy.8 = f32[2,2,16,8,1024]{4,3,2,1,0:T(8,128)} copy(f32[2,2,16,8,1024]{4,3,2,1,0:T(8,128)S(1)} %bitcast.3) | data formatting | bytes 4194304

commit v5 on v4

--- a/solution.py
+++ b/solution.py
@@ -73,6 +73,19 @@
     kap = (x + y) % 4
     cb0 = y * 2 + core
 
+    table_copy = pltpu.make_async_copy(table_ref, table, ksem)
+    tiles_copy = pltpu.make_async_copy(tiles_ref, tiles, tsem)
+
+    barrier = pltpu.get_barrier_semaphore()
+
+    @pl.loop(0, 64)
+    def _(i):
+        r = (rad + i) % 64
+
+        @pl.when(jnp.logical_or(r != rad, kap != zlo))
+        def _():
+            pl.semaphore_signal(barrier, 1, device_id=(kap, r), device_id_type=MESH)
+
     for p in range(2):
         for part in range(2):
             i = part * 2 + p
@@ -80,18 +93,6 @@
                 pltpu.make_async_copy(
                     x_ref.at[i, :, pl.ds(cb * TILE, TILE)], xin.at[i, cb], xsem.at[i]
                 ).start()
-    table_copy = pltpu.make_async_copy(table_ref, table, ksem)
-    tiles_copy = pltpu.make_async_copy(tiles_ref, tiles, tsem)
-
-    barrier = pltpu.get_barrier_semaphore()
-
-    @pl.loop(0, 64)
-    def _(i):
-        r = (rad + i) % 64
-
-        @pl.when(jnp.logical_or(r != rad, kap != zlo))
-        def _():
-            pl.semaphore_signal(barrier, 1, device_id=(kap, r), device_id_type=MESH)
 
     @pl.loop(1, 8)
     def _(i):
@@ -313,14 +314,16 @@
             to_lhs(cb, value)
 
         for degree in range(1, TAYLOR + 1):
-            @pl.loop(0, NT, unroll=NT)
-            def _(position):
+            carried = jnp.zeros((TILE, TILE), F32)
+            for position in range(NT):
                 product = jnp.dot(
                     lhs[src[position]], tile_rhs[position], preferred_element_type=F32
                 )
                 scaled = product.reshape(16, 8, TILE) * rwb[half, j, wrow[position]][None]
-                carried = jnp.where(same[position] == 1, sums[position], 0.0)
-                sums[position + 1] = scaled.reshape(TILE, TILE) + carried
+                if position:
+                    carried = jnp.where(same[position] == 1, carried, 0.0)
+                carried = scaled.reshape(TILE, TILE) + carried
+                sums[position + 1] = carried
 
             @pl.loop(0, CB)
             def _(cb):

time: 123 us -> 123 us (level)
  no operation moved by 1% of the time
where the time goes in v5:
time: 123 us
  Pallas kernels  122 us (99%)
  local copies, waits for them, and re-layouts  1.32 us (1%)
    pallas_call x1, Pallas kernels, step(): pl.pallas_call(kernel, out_shape=pltpu.VMEM(flat.shape, F32), in_specs=[a...  122 us

profile of v5, /device:TPU:1, one launch (start us, length us, event | category | flops | bytes accessed | tf_op | source)
XLA Modules:
  0.0 122.9 jit_solution(11938865996321670530)
XLA Ops:
  0.0 121.6 %wavepacket_step.1 = f32[4,128,1024]{2,1,0:T(8,128)S(1)} custom-call(f32[4,128,1024]{2,1,0:T(8,128)} %bitcast.4, f32[8,16]{1,0:T(8,128)} %weight_ref.1, f32[24,128,128]{2,1,0:T(8,128)} %tiles_ref.1, s32[3,24]{1,0:T(4,128)} %bitcast.5, f32[8,1024]{1,0:T(8,128)} %coupling_ref.1, bf16[2,2,4,256,512]{4,3,2,1,0:T(8,128)(2,1)} %constant.2.clone.table_ref), custom_call_target="tpu_custom_call" | custom-call | tf_op jit(solution)/shard_map/wavepacket_step/pallas_call | solution.py:407
  121.6 1.3 %copy.8 = f32[2,2,16,8,1024]{4,3,2,1,0:T(8,128)} copy(f32[2,2,16,8,1024]{4,3,2,1,0:T(8,128)S(1)} %bitcast.3) | data formatting | bytes 4194304
